TPU v7x, 32 devices: a whole 2x2x4 slice. The times are simulated.
32 devices in a mesh: dp: 8 (over z, core), space: 4 (over y, x).
Axes of the slice: x: 2, y: 2, z: 4, core: 2. Of those that a mesh axis runs over, the one named last changes fastest.
Arguments:
- inputs: bfloat16 [8, 24, 32, 32, 256], P('dp', 'space'), may hold values from -6 to 6
- kernels: bfloat16 [2, 3, 3, 256, 256], P(None, None, None, 'dp'), may hold values from -0.125 to 0.125
- cotangent: bfloat16 [8, 24, 32, 32, 256], P('dp', 'space'), may hold values from -0.01171875 to 0.01171875
- adjacency: int32 [24, 4, 3], P('space'), may hold values from 0 to 23, as said below
Outputs:
- final_state: bfloat16 [8, 24, 32, 32, 256], P('dp', 'space')
- kernel_grads: float32 [2, 3, 3, 256, 256], P(None, None, None, 'dp')
Inputs may be any that keep to these rules, and one draw needn't show every extreme that they name: Entry [t, e] = (n, f, r): edge e of tile t meets edge f of tile n, and r = 1 where the two edges are read in opposite directions along the shared line. The relation is symmetric: adjacency[n, f] = (t, e, r). The tiles form 2 x 2 blocks on the six faces of a cube, numbered in an order drawn from the seed.
All inputs are finite; a program needn't handle non-finite values.
Results may differ from a plain program's by a relative error of at most 0.005.
Values may be sent and summed in bfloat16 or wider, within the bound.
A program may use at most 192 MiB of HBM per device.

v0:
```python
import jax
import jax.numpy as jnp
from jax import lax
from jax.sharding import PartitionSpec as P

LAYERS = 2


def edge_strips(tile_field):
    return jnp.stack(
        [
            tile_field[:, :, 0],
            tile_field[:, :, -1],
            tile_field[:, :, :, 0],
            tile_field[:, :, :, -1],
        ],
        axis=2,
    )


def orient(strips, adjacency):
    selected = strips[:, adjacency[:, :, 0], adjacency[:, :, 1]]
    flipped = (adjacency[:, :, 2] == 1)[None, :, :, None, None]
    return jnp.where(flipped, selected[:, :, :, ::-1], selected)


def neighbor_rims(tile_field, adjacency):
    gathered = lax.all_gather(edge_strips(tile_field), "space", axis=1, tiled=True)
    return orient(gathered, adjacency)


def returned_rims(rim_values, adjacency):
    gathered = lax.all_gather(rim_values, "space", axis=1, tiled=True)
    return orient(gathered, adjacency)


def with_rim(tile_field, rim_rows):
    middle = jnp.concatenate(
        [rim_rows[:, :, 2][:, :, :, None], tile_field, rim_rows[:, :, 3][:, :, :, None]], axis=3
    )
    corner = jnp.zeros(tile_field.shape[:2] + (1, tile_field.shape[4]), tile_field.dtype)
    top_row = jnp.concatenate([corner, rim_rows[:, :, 0], corner], axis=2)[:, :, None]
    bottom_row = jnp.concatenate([corner, rim_rows[:, :, 1], corner], axis=2)[:, :, None]
    return jnp.concatenate([top_row, middle, bottom_row], axis=2)


def convolve(padded, kernel):
    extent = padded.shape[2] - 2
    channels = padded.shape[-1]
    summed = jnp.zeros(padded.shape[:2] + (extent, extent, kernel.shape[-1]), jnp.float32)
    for row_off in range(3):
        for col_off in range(3):
            patches = padded[:, :, row_off : row_off + extent, col_off : col_off + extent].reshape(
                -1, channels
            )
            summed = summed + jnp.dot(
                patches, kernel[row_off, col_off], preferred_element_type=jnp.float32
            ).reshape(summed.shape)
    return summed


def weight_grad(padded, flat_grad):
    extent = padded.shape[2] - 2
    channels = padded.shape[-1]
    rows_out = []
    for row_off in range(3):
        row_list = []
        for col_off in range(3):
            patches = padded[:, :, row_off : row_off + extent, col_off : col_off + extent].reshape(
                -1, channels
            )
            row_list.append(
                lax.dot_general(
                    patches, flat_grad, (((0,), (0,)), ((), ())), preferred_element_type=jnp.float32
                )
            )
        rows_out.append(jnp.stack(row_list))
    return jnp.stack(rows_out)


def input_grad(flat_grad, kernel, padded_shape):
    extent = padded_shape[2] - 2
    full = extent + 2
    channels = padded_shape[4]
    grid_grad = flat_grad.reshape(padded_shape[:2] + (extent, extent, flat_grad.shape[-1]))
    widened = jnp.pad(grid_grad, ((0, 0), (0, 0), (2, 2), (2, 2), (0, 0)))
    pad_grad = jnp.zeros(padded_shape, jnp.float32)
    for row_off in range(3):
        for col_off in range(3):
            window = widened[
                :, :, 2 - row_off : 2 - row_off + full, 2 - col_off : 2 - col_off + full
            ].reshape(-1, flat_grad.shape[-1])
            contrib = lax.dot_general(
                window,
                kernel[row_off, col_off],
                (((1,), (1,)), ((), ())),
                preferred_element_type=jnp.float32,
            )
            pad_grad = pad_grad + contrib.reshape(padded_shape[:4] + (channels,))
    return pad_grad


def rim_strips(pad_grad):
    return jnp.stack(
        [
            pad_grad[:, :, 0, 1:-1],
            pad_grad[:, :, -1, 1:-1],
            pad_grad[:, :, 1:-1, 0],
            pad_grad[:, :, 1:-1, -1],
        ],
        axis=2,
    )


def add_rim(interior, returned):
    interior = jnp.concatenate(
        [
            interior[:, :, :1] + returned[:, :, 0][:, :, None],
            interior[:, :, 1:-1],
            interior[:, :, -1:] + returned[:, :, 1][:, :, None],
        ],
        axis=2,
    )
    interior = jnp.concatenate(
        [
            interior[:, :, :, :1] + returned[:, :, 2][:, :, :, None],
            interior[:, :, :, 1:-1],
            interior[:, :, :, -1:] + returned[:, :, 3][:, :, :, None],
        ],
        axis=3,
    )
    return interior


def reduce_grad(partial_value):
    space_total = lax.psum(partial_value, "space")
    return lax.psum_scatter(space_total, "dp", scatter_dimension=2, tiled=True)


def per_device(inputs, kernels, cotangent, adjacency):
    weights = lax.all_gather(kernels, "dp", axis=3, tiled=True)
    current = inputs
    stored = []
    for layer_num in range(LAYERS):
        padded = with_rim(current, neighbor_rims(current, adjacency))
        preact = convolve(padded, weights[layer_num])
        current = (current.astype(jnp.float32) + jax.nn.silu(preact)).astype(jnp.bfloat16)
        stored.append((padded, preact))
    upstream = cotangent.astype(jnp.float32)
    kernel_grads = [None] * LAYERS
    for layer_num in range(LAYERS - 1, -1, -1):
        padded, preact = stored[layer_num]
        logistic = jax.nn.sigmoid(preact)
        pre_grad = (upstream * logistic * (1.0 + preact * (1.0 - logistic))).astype(jnp.bfloat16)
        flat_grad = pre_grad.reshape(-1, pre_grad.shape[-1])
        kernel_grads[layer_num] = reduce_grad(weight_grad(padded, flat_grad))
        if layer_num > 0:
            pad_grad = input_grad(flat_grad, weights[layer_num], padded.shape)
            rim_values = rim_strips(pad_grad).astype(jnp.bfloat16)
            returned = returned_rims(rim_values, adjacency).astype(jnp.float32)
            upstream = add_rim(upstream + pad_grad[:, :, 1:-1, 1:-1], returned)
    return (current, jnp.stack(kernel_grads))


def solution(mesh):
    in_specs = (
        P("dp", "space", None, None, None),
        P(None, None, None, "dp", None),
        P("dp", "space", None, None, None),
        P("space", None, None),
    )
    out_specs = (P("dp", "space", None, None, None), P(None, None, None, "dp", None))
    return jax.shard_map(
        per_device, mesh=mesh, in_specs=in_specs, out_specs=out_specs, check_vma=False
    )
```

profile of v0, /device:TPU:0, one launch (start us, length us, event | category | flops | bytes accessed | tf_op | source)
XLA Modules:
  0.0 505.8 jit_solution(17748328288666397905)
XLA Ops:
  7.2 3.8 copy.101
  12.9 32.7 %all-gather.5.cloned.1.call-done = bf16[1,24,4,32,256]{4,3,1,2,0:T(8,128)(2,1)} async-done(((bf16[1,6,4,32,256]{4,3,1,2,0:T(8,128)(2,1)}), bf16[1,24,4,32,256]{4,3,1,2,0:T(8,128)(2,1)}) %all-gather.5.cloned.1.call-update) | async-done | bytes 1572880 | tf_op jit(solution)/shard_map/all_gather | solution.py:28
  51.8 5.4 %fusion.38 = (bf16[6,32,32,256]{3,2,1,0:T(8,128)(2,1)}, bf16[6,32,32,256]{3,2,1,0:T(8,128)(2,1)}) fusion(bf16[1,6,32,32,256]{4,3,2,1,0:T(8,128)(2,1)S(1)} %copy-done.4, bf16[1,6,32,1,256]{4,3,2,1,0:T(2,128)(2,1)S(1)} %copy.109, bf16[1,6,32,1,256]{4,3,2,1,0:T(2,128)(2,1)S(1)} %copy.110), kind=kLoop, calls=%fused_computation.68 | loop fusion | flops 12582912 | bytes 9633792 | tf_op jit(solution)/shard_map/dot_general | solution.py:56
  57.2 4.9 maximum_maximum_fusion.1
  65.4 10.3 %slice_bitcast_fusion.9 = (bf16[6,32,32,256]{3,2,1,0:T(8,128)(2,1)}, bf16[6,32,32,256]{3,2,1,0:T(8,128)(2,1)}, bf16[6,32,32,256]{3,2,1,0:T(8,128)(2,1)}, bf16[6,...) fusion(bf16[1,6,33,34,256]{4,3,2,1,0:T(8,128)(2,1)S(1)} %get-tuple-element.31, ...), kind=kLoop, calls=%fused_computation.64 | loop fusion | bytes 37748736 | tf_op jit(solution)/shard_map/dot_general | solution.py:56
  75.8 3.0 all-gather.7.cloned.1.call-done
  78.7 3.0 slice_bitcast_fusion.14
  81.7 6.2 %fusion.60 = f32[6,32,32,256]{3,1,0,2:T(8,128)} fusion(bf16[6,32,32,256]{3,2,1,0:T(8,128)(2,1)S(1)} %copy-done.18, bf16[3,3,256,256]{3,2,1,0:T(8,128)(2,1)S(1)} %get-tuple-element.46), kind=kOutput, calls=%fused_computation.93 | convolution fusion | flops 805306368 | bytes 9568256 | tf_op jit(solution)/shard_map/dot_general | solution.py:56
  88.0 6.2 %fusion.62 = f32[6,32,32,256]{3,1,0,2:T(8,128)} fusion(bf16[6,32,32,256]{3,2,1,0:T(8,128)(2,1)S(1)} %copy-done.17, bf16[3,3,256,256]{3,2,1,0:T(8,128)(2,1)S(1)} %get-tuple-element.46), kind=kOutput, calls=%fused_computation.95 | convolution fusion | flops 805306368 | bytes 9568256 | tf_op jit(solution)/shard_map/dot_general | solution.py:56
  94.2 6.3 %fusion.64 = f32[6,32,32,256]{3,1,0,2:T(8,128)} fusion(bf16[6,32,32,256]{3,2,1,0:T(8,128)(2,1)S(1)} %copy-done.16, bf16[3,3,256,256]{3,2,1,0:T(8,128)(2,1)S(1)} %get-tuple-element.46), kind=kOutput, calls=%fused_computation.97 | convolution fusion | flops 805306368 | bytes 9568256 | tf_op jit(solution)/shard_map/dot_general | solution.py:56
  100.5 6.4 %fusion.66 = f32[6,32,32,256]{3,1,0,2:T(8,128)} fusion(bf16[6,32,32,256]{3,2,1,0:T(8,128)(2,1)S(1)} %copy-done.21, bf16[3,3,256,256]{3,2,1,0:T(8,128)(2,1)S(1)} %get-tuple-element.46), kind=kOutput, calls=%fused_computation.99 | convolution fusion | flops 805306368 | bytes 9568256 | tf_op jit(solution)/shard_map/dot_general | solution.py:56
  106.9 6.3 %fusion.68 = f32[6,32,32,256]{3,1,0,2:T(8,128)} fusion(bf16[6,32,32,256]{3,2,1,0:T(8,128)(2,1)S(1)} %bitcast.431, bf16[3,3,256,256]{3,2,1,0:T(8,128)(2,1)S(1)} %get-tuple-element.46), kind=kOutput, calls=%fused_computation.101 | convolution fusion | flops 805306368 | bytes 9568256 | tf_op jit(solution)/shard_map/dot_general | solution.py:56
  113.1 6.2 %fusion.70 = f32[6,32,32,256]{3,1,0,2:T(8,128)} fusion(bf16[6,32,32,256]{3,2,1,0:T(8,128)(2,1)S(1)} %copy-done.19, bf16[3,3,256,256]{3,2,1,0:T(8,128)(2,1)S(1)} %get-tuple-element.46), kind=kOutput, calls=%fused_computation.103 | convolution fusion | flops 805306368 | bytes 9568256 | tf_op jit(solution)/shard_map/dot_general | solution.py:56
  119.4 6.7 %fusion.72 = f32[6,32,32,256]{3,1,0,2:T(8,128)} fusion(bf16[6,32,32,256]{3,2,1,0:T(8,128)(2,1)S(1)} %copy-done.15, bf16[3,3,256,256]{3,2,1,0:T(8,128)(2,1)S(1)} %get-tuple-element.46), kind=kOutput, calls=%fused_computation.105 | convolution fusion | flops 805306368 | bytes 9568256 | tf_op jit(solution)/shard_map/dot_general | solution.py:56
  126.1 6.2 %fusion.74 = f32[6,32,32,256]{3,1,0,2:T(8,128)} fusion(bf16[6,32,32,256]{3,2,1,0:T(8,128)(2,1)S(1)} %copy-done.14, bf16[3,3,256,256]{3,2,1,0:T(8,128)(2,1)S(1)} %get-tuple-element.46), kind=kOutput, calls=%fused_computation.107 | convolution fusion | flops 805306368 | bytes 9568256 | tf_op jit(solution)/shard_map/dot_general | solution.py:56
  132.3 22.0 %fusion.5 = (bf16[1,6,32,32,256]{4,2,1,3,0:T(8,128)(2,1)S(1)}, f32[6,32,32,256]{3,1,0,2:T(8,128)}) fusion(bf16[1,6,32,32,256]{4,3,2,1,0:T(8,128)(2,1)S(1)} %copy-done.5, f32[6,32,32,256]{3,1,0,2:T(8,128)} %fusion.60, f32[6,32,32,256]{3,1,0,2:T(8,128)} %fusion.62, f32[6,32,32,256]{3,1,0,2:T(8,128)} %fusion.64, f32[6,32,32,256]{3,1,0,2:T(8,128)} %fusion.66, ...), kind=kOutput, calls=%fused_computation.15 | convolution fusion | flops 828899328 | bytes 66191360 | tf_op jit(solution)/shard_map/dot_general | solution.py:56
  155.9 4.5 fusion.141
  160.4 25.7 %all-gather.9.cloned.1.call-done = bf16[1,24,4,32,256]{4,3,1,2,0:T(8,128)(2,1)} async-done(((bf16[1,6,4,32,256]{4,3,1,2,0:T(8,128)(2,1)}), bf16[1,24,4,32,256]{4,3,1,2,0:T(8,128)(2,1)}) %all-gather.9.cloned.1.call-update) | async-done | bytes 1572880 | tf_op jit(solution)/shard_map/all_gather | solution.py:28
  192.5 2.9 maximum_maximum_fusion
  195.4 4.0 fusion.144
  199.4 3.6 fusion.143
  203.5 4.1 fusion.139
  207.6 3.6 fusion.137
  211.3 3.7 fusion.138
  214.9 7.1 %slice_bitcast_fusion.3 = (bf16[6,32,32,256]{3,1,0,2:T(8,128)(2,1)}, bf16[6,32,32,256]{3,1,0,2:T(8,128)(2,1)}, bf16[6,32,32,256]{3,1,0,2:T(8,128)(2,1)}) fusion(bf16[1,6,33,34,256]{4,2,1,3,0:T(8,128)(2,1)S(1)} %get-tuple-element.33), kind=kLoop, calls=%fused_computation.54 | loop fusion | bytes 18874368 | tf_op jit(solution)/shard_map/dot_general | solution.py:56
  222.1 3.6 fusion.142
  225.6 3.7 fusion.140
  229.3 21.6 %fusion.1 = (bf16[1,6,32,32,256]{4,2,1,3,0:T(8,128)(2,1)S(1)}, bf16[1,6,32,32,256]{4,2,1,3,0:T(8,128)(2,1)}) fusion(bf16[1,6,32,32,256]{4,3,2,1,0:T(8,128)(2,1)} %param.6, bf16[1,6,32,32,256]{4,2,1,3,0:T(8,128)(2,1)} %copy-done.2, bf16[3,3,256,256]{3,2,1,0:T(8,128)(2,1)} %get-tuple-element.47, bf16[1,6,33,34,256]{4,2,1,3,0:T(8,128)(2,1)S(1)} %get-tuple-element.33, ...), kind=kOutput, calls=%fused_computation.7 | convolution fusion | flops 839909376 | bytes 66191360 | tf_op jit(solution)/shard_map/dot_general | solution.py:56
  250.9 3.8 fusion.100
  258.9 4.3 slice_bitcast_fusion.6
  263.1 4.6 fusion.28
  267.7 4.7 fusion.25
  272.4 4.6 fusion.22
  277.0 4.7 fusion.19
  281.7 4.6 fusion.16
  286.3 4.6 fusion.13
  290.8 4.6 fusion.7
  295.5 4.6 fusion.10
  300.1 27.1 %fusion.164 = (bf16[1,6,34,34,256]{4,2,1,3,0:T(8,128)(2,1)}, f32[1,6,34,34,256]{4,2,1,3,0:T(8,128)}) fusion(bf16[3,3,256,256]{3,2,1,0:T(8,128)(2,1)} %get-tuple-element.47, bf16[1,6,32,32,256]{4,2,1,3,0:T(8,128)(2,1)S(1)} %get-tuple-element.12, f32[6,34,34,256]{3,1,0,2:T(8,128)} %fusion.28, f32[6,34,34,256]{3,1,0,2:T(8,128)} %fusion.25, ...), kind=kOutput, calls=%fused_computation.247 | convolution fusion | flops 925095936 | bytes 80777216 | tf_op jit(solution)/shard_map/dot_general | solution.py:93
  329.9 3.8 fusion.109
  340.1 6.4 %convert_add_fusion = f32[1,6,32,32,256]{4,2,1,3,0:T(8,128)S(1)} fusion(f32[1,6,34,34,256]{4,2,1,3,0:T(8,128)} %get-tuple-element.65, bf16[1,6,32,32,256]{4,3,2,1,0:T(8,128)(2,1)} %param.6), kind=kLoop, calls=%fused_computation.4 | loop fusion | flops 3145728 | bytes 15728640 | tf_op jit(solution)/shard_map/add | solution.py:161
  346.6 3.6 slice.427
  357.7 13.4 %all-gather.11.cloned.1.call-done = bf16[1,24,4,32,256]{4,3,1,2,0:T(8,128)(2,1)} async-done(((bf16[1,6,4,32,256]{4,3,1,2,0:T(8,128)(2,1)}), bf16[1,24,4,32,256]{4,3,1,2,0:T(8,128)(2,1)}) %all-gather.11.cloned.1.call-update) | async-done | bytes 1572880 | tf_op jit(solution)/shard_map/all_gather | solution.py:33
  379.6 2.6 fusion.3
  405.5 5.4 %reduce-scatter.5.cloned.1.call-done = f32[3,3,32,256]{3,2,1,0:T(8,128)} async-done(((f32[3,3,256,256]{3,2,1,0:T(8,128)}), f32[3,3,32,256]{3,2,1,0:T(8,128)}) %reduce-scatter.5.cloned.1.call-update) | async-done | bytes 294928 | tf_op jit(solution)/shard_map/reduce_scatter | solution.py:137
  410.8 38.1 %reduce-scatter.3.cloned.1.call-done = f32[3,3,32,256]{3,2,1,0:T(8,128)} async-done(((f32[3,3,256,256]{3,2,1,0:T(8,128)}), f32[3,3,32,256]{3,2,1,0:T(8,128)}) %reduce-scatter.3.cloned.1.call-update) | async-done | bytes 294928 | tf_op jit(solution)/shard_map/reduce_scatter | solution.py:137
  449.0 3.5 copy.200
  452.5 44.4 %all-reduce.4.cloned.1.call-done = (f32[3,3,32,256]{3,2,1,0:T(8,128)}, f32[3,3,32,256]{3,2,1,0:T(8,128)}) async-done(((f32[3,3,32,256]{3,2,1,0:T(8,128)}, f32[3,3,32,256]{3,2,1,0:T(8,128)}), (f32[3,3,32,256]{3,2,1,0:T(8,128)}, f32[3,3,32,256]{3,2,1,0:T(8,128)})) %all-reduce.4.cloned.1.call-update) | async-done | bytes 589840 | tf_op jit(solution)/shard_map/psum | solution.py:136
  (175 shorter events, 73.8 us)
Async XLA Ops:
  7.2 3.9 copy-start.4
  7.2 5.6 %copy-start.40 = (s32[6,4,3]{0,1,2:T(4,128)S(1)}, s32[6,4,3]{0,1,2:T(4,128)}, u32[]{:S(2)}) copy-start(s32[6,4,3]{0,1,2:T(4,128)} %param.7) | copy-start | bytes 868
  7.2 38.5 %all-gather.5.cloned.1.call-start = ((), (), s32[]{:S(2)}) async-start(), calls=%async_computation.2 | async-start | bytes 1966080 | tf_op jit(solution)/shard_map/all_gather | solution.py:28
  11.9 66.8 %all-gather.7.cloned.1.call-start = ((), (), s32[]{:S(2)}) async-start(), calls=%async_computation.3 | async-start | bytes 2654208 | tf_op jit(solution)/shard_map/all_gather | solution.py:141
  12.7 173.4 %all-gather.9.cloned.1.call-start = ((), (), s32[]{:S(2)}) async-start(), calls=%async_computation.4 | async-start | bytes 1966080 | tf_op jit(solution)/shard_map/all_gather | solution.py:28
  62.1 2.1 copy-start.7
  62.1 3.3 copy-start.9
  78.7 3.0 copy-start.18
  81.7 6.2 %copy-start.17 = (bf16[6,32,32,256]{3,2,1,0:T(8,128)(2,1)S(1)}, bf16[6,32,32,256]{3,2,1,0:T(8,128)(2,1)}, u32[]{:S(2)}) copy-start(bf16[6,32,32,256]{3,2,1,0:T(8,128)(2,1)} %get-tuple-element.29) | copy-start | bytes 9437188
  88.0 6.2 %copy-start.16 = (bf16[6,32,32,256]{3,2,1,0:T(8,128)(2,1)S(1)}, bf16[6,32,32,256]{3,2,1,0:T(8,128)(2,1)}, u32[]{:S(2)}) copy-start(bf16[6,32,32,256]{3,2,1,0:T(8,128)(2,1)} %get-tuple-element.27) | copy-start | bytes 9437188
  94.2 6.3 %copy-start.21 = (bf16[6,32,32,256]{3,2,1,0:T(8,128)(2,1)S(1)}, bf16[6,32,32,256]{3,2,1,0:T(8,128)(2,1)}, u32[]{:S(2)}) copy-start(bf16[6,32,32,256]{3,2,1,0:T(8,128)(2,1)} %get-tuple-element.41) | copy-start | bytes 9437188
  106.9 6.3 %copy-start.19 = (bf16[6,32,32,256]{3,2,1,0:T(8,128)(2,1)S(1)}, bf16[6,32,32,256]{3,2,1,0:T(8,128)(2,1)}, u32[]{:S(2)}) copy-start(bf16[6,32,32,256]{3,2,1,0:T(8,128)(2,1)} %get-tuple-element.40) | copy-start | bytes 9437188
  113.1 6.3 %copy-start.15 = (bf16[6,32,32,256]{3,2,1,0:T(8,128)(2,1)S(1)}, bf16[6,32,32,256]{3,2,1,0:T(8,128)(2,1)}, u32[]{:S(2)}) copy-start(bf16[6,32,32,256]{3,2,1,0:T(8,128)(2,1)} %get-tuple-element.67) | copy-start | bytes 9437188
  119.4 6.7 %copy-start.14 = (bf16[6,32,32,256]{3,2,1,0:T(8,128)(2,1)S(1)}, bf16[6,32,32,256]{3,2,1,0:T(8,128)(2,1)}, u32[]{:S(2)}) copy-start(bf16[6,32,32,256]{3,2,1,0:T(8,128)(2,1)} %get-tuple-element.66) | copy-start | bytes 9437188
  126.1 6.2 %copy-start.5 = (bf16[1,6,32,32,256]{4,3,2,1,0:T(8,128)(2,1)S(1)}, bf16[1,6,32,32,256]{4,3,2,1,0:T(8,128)(2,1)}, u32[]{:S(2)}) copy-start(bf16[1,6,32,32,256]{4,3,2,1,0:T(8,128)(2,1)} %param.4) | copy-start | bytes 9437188
  126.1 6.2 %copy-start.12 = (bf16[6,32,32,256]{3,2,1,0:T(8,128)(2,1)S(1)}, bf16[6,32,32,256]{3,2,1,0:T(8,128)(2,1)}, u32[]{:S(2)}) copy-start(bf16[6,32,32,256]{3,2,1,0:T(8,128)(2,1)} %get-tuple-element.68) | copy-start | bytes 9437188
  154.4 48.6 %copy-start.2 = (bf16[1,6,32,32,256]{4,2,1,3,0:T(8,128)(2,1)}, bf16[1,6,32,32,256]{4,2,1,3,0:T(8,128)(2,1)S(1)}, u32[]{:S(2)}) copy-start(bf16[1,6,32,32,256]{4,2,1,3,0:T(8,128)(2,1)S(1)} %get-tuple-element.62) | copy-start | bytes 9437188
  155.9 215.2 %all-gather.11.cloned.1.call-start = ((), (), s32[]{:S(2)}) async-start(), calls=%async_computation.5 | async-start | bytes 1966080 | tf_op jit(solution)/shard_map/all_gather | solution.py:33
  192.4 2.9 copy-start.26
  195.4 15.9 %copy-start = (bf16[1,6,33,34,256]{4,2,1,3,0:T(8,128)(2,1)}, bf16[1,6,33,34,256]{4,2,1,3,0:T(8,128)(2,1)S(1)}, u32[]{:S(2)}) copy-start(bf16[1,6,33,34,256]{4,2,1,3,0:T(8,128)(2,1)S(1)} %get-tuple-element.32) | copy-start | bytes 10340356
  203.5 18.5 %copy-start.25 = (bf16[6,32,32,256]{3,1,0,2:T(8,128)(2,1)}, bf16[6,32,32,256]{3,1,0,2:T(8,128)(2,1)S(1)}, u32[]{:S(2)}) copy-start(bf16[6,32,32,256]{3,1,0,2:T(8,128)(2,1)S(1)} %get-tuple-element.35) | copy-start | bytes 9437188
  203.5 22.1 %copy-start.23 = (bf16[6,32,32,256]{3,1,0,2:T(8,128)(2,1)}, bf16[6,32,32,256]{3,1,0,2:T(8,128)(2,1)S(1)}, u32[]{:S(2)}) copy-start(bf16[6,32,32,256]{3,1,0,2:T(8,128)(2,1)S(1)} %get-tuple-element.34) | copy-start | bytes 9437188
  250.9 3.8 copy-start.3
  254.7 1.9 copy-start.24
  256.6 2.3 copy-start.1
  258.9 4.3 copy-start.27
  329.9 3.8 copy-start.31
  340.1 70.8 %reduce-scatter.5.cloned.1.call-start = ((), (), s32[]{:S(2)}) async-start(), calls=%async_computation.7 | async-start | bytes 2654208 | tf_op jit(solution)/shard_map/reduce_scatter | solution.py:137
  346.5 4.6 copy-start.11
  346.5 4.6 copy-start.37
  346.5 4.6 copy-start.38
  346.6 4.6 copy-start.39
  346.6 4.6 copy-start.33
  346.6 4.6 copy-start.34
  346.6 4.6 copy-start.35
  351.1 1.9 copy-start.29
  357.6 19.9 %slice-start = ((s8[6291456]{0:T(1024)(128)(4,1)}), s8[2097152]{0:T(1024)(128)(4,1)S(1)}, s32[]{:S(2)}) async-start(s8[6291456]{0:T(1024)(128)(4,1)} %bitcast.433), calls=%async_computation.9 | async-start | bytes 4194304
  357.6 91.3 %reduce-scatter.3.cloned.1.call-start = ((), (), s32[]{:S(2)}) async-start(), calls=%async_computation.6 | async-start | bytes 2654208 | tf_op jit(solution)/shard_map/reduce_scatter | solution.py:137
  373.6 3.9 slice-start.1
  376.2 3.4 slice-start.2
  377.5 2.1 slice-start.3
  379.6 2.7 copy-start.10
  387.3 2.3 copy-start.6
  389.6 2.5 copy-start.22
  392.1 2.2 copy-start.20
  394.3 2.4 copy-start.8
  403.8 45.1 %copy-start.13 = (bf16[1,6,32,32,256]{4,2,1,3,0:T(8,128)(2,1)S(1)}, bf16[1,6,32,32,256]{4,2,1,3,0:T(8,128)(2,1)}, u32[]{:S(2)}) copy-start(bf16[1,6,32,32,256]{4,2,1,3,0:T(8,128)(2,1)} %get-tuple-element.13) | copy-start | bytes 9437188
  405.4 91.5 %all-reduce.4.cloned.1.call-start = ((), (), s32[]{:S(2)}) async-start(), calls=%async_computation.8 | async-start | bytes 1179648 | tf_op jit(solution)/shard_map/psum | solution.py:136
  (4 other events, 6.7 us)
Sparse Core Ops, SparseCore 0:
  12.0 33.5 all-gather.4
  47.2 31.4 all-gather.6
  156.0 30.0 all-gather.8
  340.2 30.8 all-gather.10
  373.8 36.9 reduce-scatter.4
  413.0 35.8 reduce-scatter.2
  451.9 44.9 all-reduce.3
where the time goes:
time: 513 us; the launch traced here: 506 us
  matrix products  228 us (44%)
  waiting for transfers between devices  163 us (32%)
  local copies, waits for them, and re-layouts  60.5 us (12%)
  other arithmetic  38.2 us (7%)
  between operations  15.1 us (3%)
    dot_general x18, matrix products, convolve(): jnp.dot(patches, kernel[row_off, col_off], preferred_element_type=jnp.flo...  125 us
    dot_general x9, matrix products, input_grad(): lax.dot_general(window, kernel[row_off, col_off], (((1,), (1,)), ((), ())...  64 us
    all_gather x2, waiting for transfers between devices, neighbor_rims(): lax.all_gather(edge_strips(tile_field), 'space', axis=1, tiled=True)  58.4 us
    psum x1, waiting for transfers between devices, reduce_grad(): space_total = lax.psum(partial_value, 'space')  44.4 us
    reduce_scatter x2, waiting for transfers between devices, reduce_grad(): return lax.psum_scatter(space_total, 'dp', scatter_dimension=2, tiled=True)  43.4 us
    dot_general x18, matrix products, weight_grad(): lax.dot_general(patches, flat_grad, (((0,), (0,)), ((), ())), preferred_e...  39.5 us
    dot_general x3, local copies, waits for them, and re-layouts, convolve(): jnp.dot(patches, kernel[row_off, col_off], preferred_element_type=jnp.flo...  21.7 us
    unnamed x97, local copies, waits for them, and re-layouts  15.4 us
  transfers between devices with their start and end apart: 7, of which 7 were waited for; matrix products, arithmetic and copies ran while one was open for 16% of the time, Pallas kernels for 0%

commit v1 on v0

--- a/solution.py
+++ b/solution.py
@@ -133,7 +133,10 @@
 
 
 def reduce_grad(partial_value):
-    space_total = lax.psum(partial_value, "space")
+    n_dev, space_total = (lax.axis_size("space"), partial_value)
+    for far in [1 << k for k in range(n_dev.bit_length() - 1)]:
+        pairs = [(i, i ^ far) for i in range(n_dev)]
+        space_total = space_total + lax.ppermute(space_total, "space", pairs)
     return lax.psum_scatter(space_total, "dp", scatter_dimension=2, tiled=True)
 
 

time: 513 us -> 590 us (1.15)
  waiting for transfers between devices: 163 us -> 222 us
  other arithmetic: 38.2 us -> 46.7 us
    ppermute x0 -> x4, waiting for transfers between devices: none -> 102 us  [reduce_grad(): space_total = space_total + lax.ppermute(space_total, 'space', pairs)]
    psum x1 -> x0, waiting for transfers between devices: 44.4 us -> none  [reduce_grad(): space_total = lax.psum(partial_value, 'space')]
    all_gather x1, waiting for transfers between devices: 13.4 us -> 25.3 us  [returned_rims(): gathered = lax.all_gather(rim_values, 'space', axis=1, tiled=True)]
    reduce_scatter x2, waiting for transfers between devices: 43.4 us -> 32.7 us  [reduce_grad(): return lax.psum_scatter(space_total, 'dp', scatter_dimension=2, tiled=True)]
    add x0 -> x4, other arithmetic: none -> 8.53 us  [reduce_grad(): space_total = space_total + lax.ppermute(space_total, 'space', pairs)]
    unnamed x97 -> x107, local copies, waits for them, and re-layouts: 15.4 us -> 18.9 us
  transfers between devices with their start and end apart: 7 -> 10, of which waited for: 7 -> 8; matrix products, arithmetic and copies ran while one was open for 16% -> 16% of each run, Pallas kernels for 0% -> 0%
where the time goes in v1:
time: 590 us; the launch traced here: 582 us
  matrix products  228 us (39%)
  waiting for transfers between devices  222 us (38%)
  local copies, waits for them, and re-layouts  65.5 us (11%)
  other arithmetic  46.7 us (8%)
  between operations  15.1 us (3%)
    dot_general x18, matrix products, convolve(): jnp.dot(patches, kernel[row_off, col_off], preferred_element_type=jnp.flo...  125 us
    ppermute x4, waiting for transfers between devices, reduce_grad(): space_total = space_total + lax.ppermute(space_total, 'space', pairs)  102 us
    dot_general x9, matrix products, input_grad(): lax.dot_general(window, kernel[row_off, col_off], (((1,), (1,)), ((), ())...  64 us
    all_gather x2, waiting for transfers between devices, neighbor_rims(): lax.all_gather(edge_strips(tile_field), 'space', axis=1, tiled=True)  58.4 us
    dot_general x18, matrix products, weight_grad(): lax.dot_general(patches, flat_grad, (((0,), (0,)), ((), ())), preferred_e...  39.8 us
    reduce_scatter x2, waiting for transfers between devices, reduce_grad(): return lax.psum_scatter(space_total, 'dp', scatter_dimension=2, tiled=True)  32.7 us
    all_gather x1, waiting for transfers between devices, returned_rims(): gathered = lax.all_gather(rim_values, 'space', axis=1, tiled=True)  25.3 us
    dot_general x3, local copies, waits for them, and re-layouts, convolve(): jnp.dot(patches, kernel[row_off, col_off], preferred_element_type=jnp.flo...  21.7 us
  transfers between devices with their start and end apart: 10, of which 8 were waited for; matrix products, arithmetic and copies ran while one was open for 16% of the time, Pallas kernels for 0%

profile of v1, /device:TPU:0, one launch (start us, length us, event | category | flops | bytes accessed | tf_op | source)
XLA Modules:
  0.0 582.1 jit_solution(11134551720117653302)
XLA Ops:
  7.2 3.8 copy.101
  12.9 32.7 %all-gather.5.cloned.1.call-done = bf16[1,24,4,32,256]{4,3,1,2,0:T(8,128)(2,1)} async-done(((bf16[1,6,4,32,256]{4,3,1,2,0:T(8,128)(2,1)}), bf16[1,24,4,32,256]{4,3,1,2,0:T(8,128)(2,1)}) %all-gather.5.cloned.1.call-update) | async-done | bytes 1572880 | tf_op jit(solution)/shard_map/all_gather | solution.py:28
  51.8 5.4 fusion.38
  57.2 4.9 maximum_maximum_fusion.1
  65.4 10.3 %slice_bitcast_fusion.9 = (bf16[6,32,32,256]{3,2,1,0:T(8,128)(2,1)}, bf16[6,32,32,256]{3,2,1,0:T(8,128)(2,1)}, bf16[6,32,32,256]{3,2,1,0:T(8,128)(2,1)}, bf16[6,...) fusion(bf16[1,6,33,34,256]{4,3,2,1,0:T(8,128)(2,1)S(1)} %get-tuple-element.29, ...), kind=kLoop, calls=%fused_computation.64 | loop fusion | bytes 37748736 | tf_op jit(solution)/shard_map/dot_general | solution.py:56
  75.7 3.0 all-gather.7.cloned.1.call-done
  78.7 3.0 slice_bitcast_fusion.14
  81.7 6.2 %fusion.60 = f32[6,32,32,256]{3,1,0,2:T(8,128)} fusion(bf16[6,32,32,256]{3,2,1,0:T(8,128)(2,1)S(1)} %copy-done.27, bf16[3,3,256,256]{3,2,1,0:T(8,128)(2,1)S(1)} %get-tuple-element.44), kind=kOutput, calls=%fused_computation.93 | convolution fusion | flops 805306368 | bytes 9568256 | tf_op jit(solution)/shard_map/dot_general | solution.py:56
  87.9 6.2 %fusion.62 = f32[6,32,32,256]{3,1,0,2:T(8,128)} fusion(bf16[6,32,32,256]{3,2,1,0:T(8,128)(2,1)S(1)} %copy-done.26, bf16[3,3,256,256]{3,2,1,0:T(8,128)(2,1)S(1)} %get-tuple-element.44), kind=kOutput, calls=%fused_computation.95 | convolution fusion | flops 805306368 | bytes 9568256 | tf_op jit(solution)/shard_map/dot_general | solution.py:56
  94.1 6.3 %fusion.64 = f32[6,32,32,256]{3,1,0,2:T(8,128)} fusion(bf16[6,32,32,256]{3,2,1,0:T(8,128)(2,1)S(1)} %copy-done.25, bf16[3,3,256,256]{3,2,1,0:T(8,128)(2,1)S(1)} %get-tuple-element.44), kind=kOutput, calls=%fused_computation.97 | convolution fusion | flops 805306368 | bytes 9568256 | tf_op jit(solution)/shard_map/dot_general | solution.py:56
  100.4 6.4 %fusion.66 = f32[6,32,32,256]{3,1,0,2:T(8,128)} fusion(bf16[6,32,32,256]{3,2,1,0:T(8,128)(2,1)S(1)} %copy-done.30, bf16[3,3,256,256]{3,2,1,0:T(8,128)(2,1)S(1)} %get-tuple-element.44), kind=kOutput, calls=%fused_computation.99 | convolution fusion | flops 805306368 | bytes 9568256 | tf_op jit(solution)/shard_map/dot_general | solution.py:56
  106.8 6.2 %fusion.68 = f32[6,32,32,256]{3,1,0,2:T(8,128)} fusion(bf16[6,32,32,256]{3,2,1,0:T(8,128)(2,1)S(1)} %bitcast.431, bf16[3,3,256,256]{3,2,1,0:T(8,128)(2,1)S(1)} %get-tuple-element.44), kind=kOutput, calls=%fused_computation.101 | convolution fusion | flops 805306368 | bytes 9568256 | tf_op jit(solution)/shard_map/dot_general | solution.py:56
  113.1 6.2 %fusion.70 = f32[6,32,32,256]{3,1,0,2:T(8,128)} fusion(bf16[6,32,32,256]{3,2,1,0:T(8,128)(2,1)S(1)} %copy-done.28, bf16[3,3,256,256]{3,2,1,0:T(8,128)(2,1)S(1)} %get-tuple-element.44), kind=kOutput, calls=%fused_computation.103 | convolution fusion | flops 805306368 | bytes 9568256 | tf_op jit(solution)/shard_map/dot_general | solution.py:56
  119.3 6.7 %fusion.72 = f32[6,32,32,256]{3,1,0,2:T(8,128)} fusion(bf16[6,32,32,256]{3,2,1,0:T(8,128)(2,1)S(1)} %copy-done.24, bf16[3,3,256,256]{3,2,1,0:T(8,128)(2,1)S(1)} %get-tuple-element.44), kind=kOutput, calls=%fused_computation.105 | convolution fusion | flops 805306368 | bytes 9568256 | tf_op jit(solution)/shard_map/dot_general | solution.py:56
  126.0 6.2 %fusion.74 = f32[6,32,32,256]{3,1,0,2:T(8,128)} fusion(bf16[6,32,32,256]{3,2,1,0:T(8,128)(2,1)S(1)} %copy-done.23, bf16[3,3,256,256]{3,2,1,0:T(8,128)(2,1)S(1)} %get-tuple-element.44), kind=kOutput, calls=%fused_computation.107 | convolution fusion | flops 805306368 | bytes 9568256 | tf_op jit(solution)/shard_map/dot_general | solution.py:56
  132.2 22.0 %fusion.5 = (bf16[1,6,32,32,256]{4,2,1,3,0:T(8,128)(2,1)S(1)}, f32[6,32,32,256]{3,1,0,2:T(8,128)}) fusion(bf16[1,6,32,32,256]{4,3,2,1,0:T(8,128)(2,1)S(1)} %copy-done.5, f32[6,32,32,256]{3,1,0,2:T(8,128)} %fusion.60, f32[6,32,32,256]{3,1,0,2:T(8,128)} %fusion.62, f32[6,32,32,256]{3,1,0,2:T(8,128)} %fusion.64, f32[6,32,32,256]{3,1,0,2:T(8,128)} %fusion.66, ...), kind=kOutput, calls=%fused_computation.15 | convolution fusion | flops 828899328 | bytes 66191360 | tf_op jit(solution)/shard_map/dot_general | solution.py:56
  155.8 4.5 fusion.141
  160.3 25.7 %all-gather.9.cloned.1.call-done = bf16[1,24,4,32,256]{4,3,1,2,0:T(8,128)(2,1)} async-done(((bf16[1,6,4,32,256]{4,3,1,2,0:T(8,128)(2,1)}), bf16[1,24,4,32,256]{4,3,1,2,0:T(8,128)(2,1)}) %all-gather.9.cloned.1.call-update) | async-done | bytes 1572880 | tf_op jit(solution)/shard_map/all_gather | solution.py:28
  192.3 2.9 maximum_maximum_fusion
  195.2 3.9 fusion.144
  199.2 3.6 fusion.143
  203.3 4.1 fusion.139
  207.4 3.6 fusion.137
  211.0 3.6 fusion.138
  214.7 7.1 %slice_bitcast_fusion.3 = (bf16[6,32,32,256]{3,1,0,2:T(8,128)(2,1)}, bf16[6,32,32,256]{3,1,0,2:T(8,128)(2,1)}, bf16[6,32,32,256]{3,1,0,2:T(8,128)(2,1)}) fusion(bf16[1,6,33,34,256]{4,2,1,3,0:T(8,128)(2,1)S(1)} %get-tuple-element.31), kind=kLoop, calls=%fused_computation.54 | loop fusion | bytes 18874368 | tf_op jit(solution)/shard_map/dot_general | solution.py:56
  221.8 3.6 fusion.142
  225.4 3.6 fusion.140
  229.0 21.6 %fusion.1 = (bf16[1,6,32,32,256]{4,2,1,3,0:T(8,128)(2,1)S(1)}, bf16[1,6,32,32,256]{4,2,1,3,0:T(8,128)(2,1)}) fusion(bf16[1,6,32,32,256]{4,3,2,1,0:T(8,128)(2,1)} %param.6, bf16[1,6,32,32,256]{4,2,1,3,0:T(8,128)(2,1)} %copy-done.2, bf16[3,3,256,256]{3,2,1,0:T(8,128)(2,1)} %get-tuple-element.45, bf16[1,6,33,34,256]{4,2,1,3,0:T(8,128)(2,1)S(1)} %get-tuple-element.31, ...), kind=kOutput, calls=%fused_computation.7 | convolution fusion | flops 839909376 | bytes 66191360 | tf_op jit(solution)/shard_map/dot_general | solution.py:56
  250.6 3.8 fusion.100
  258.5 4.3 slice_bitcast_fusion.6
  262.8 4.5 fusion.28
  267.4 4.7 fusion.25
  272.1 4.7 fusion.22
  276.7 4.7 fusion.19
  281.4 4.6 fusion.16
  286.0 4.6 fusion.13
  290.6 4.6 fusion.7
  295.2 4.6 fusion.10
  299.8 27.0 %fusion.166 = (bf16[1,6,34,34,256]{4,2,1,3,0:T(8,128)(2,1)}, f32[1,6,34,34,256]{4,2,1,3,0:T(8,128)}) fusion(bf16[3,3,256,256]{3,2,1,0:T(8,128)(2,1)} %get-tuple-element.45, bf16[1,6,32,32,256]{4,2,1,3,0:T(8,128)(2,1)S(1)} %get-tuple-element.10, f32[6,34,34,256]{3,1,0,2:T(8,128)} %fusion.28, f32[6,34,34,256]{3,1,0,2:T(8,128)} %fusion.25, ...), kind=kOutput, calls=%fused_computation.249 | convolution fusion | flops 925095936 | bytes 80777216 | tf_op jit(solution)/shard_map/dot_general | solution.py:93
  329.6 3.8 fusion.109
  354.3 3.5 slice.427
  357.9 25.3 %all-gather.11.cloned.1.call-done = bf16[1,24,4,32,256]{4,3,1,2,0:T(8,128)(2,1)} async-done(((bf16[1,6,4,32,256]{4,3,1,2,0:T(8,128)(2,1)}), bf16[1,24,4,32,256]{4,3,1,2,0:T(8,128)(2,1)}) %all-gather.11.cloned.1.call-update) | async-done | bytes 1572880 | tf_op jit(solution)/shard_map/all_gather | solution.py:33
  426.0 44.4 %collective-permute-done.3 = f32[3,3,256,256]{3,2,1,0:T(8,128)S(1)} collective-permute-done((f32[3,3,256,256]{3,2,1,0:T(8,128)S(1)}, f32[3,3,256,256]{3,2,1,0:T(8,128)S(1)}, u32[]{:S(2)}, u32[]{:S(2)}) %collective-permute-start.3) | collective-permute-done | bytes 2359328 | tf_op jit(solution)/shard_map/ppermute | solution.py:139
  472.6 5.9 %collective-permute-done = f32[3,3,256,256]{3,2,1,0:T(8,128)} collective-permute-done((f32[3,3,256,256]{3,2,1,0:T(8,128)}, f32[3,3,256,256]{3,2,1,0:T(8,128)}, u32[]{:S(2)}, u32[]{:S(2)}) %collective-permute-start) | collective-permute-done | bytes 2359328 | tf_op jit(solution)/shard_map/ppermute | solution.py:139
  481.3 51.2 %collective-permute-done.1 = f32[3,3,256,256]{3,2,1,0:T(8,128)S(1)} collective-permute-done((f32[3,3,256,256]{3,2,1,0:T(8,128)S(1)}, f32[3,3,256,256]{3,2,1,0:T(8,128)S(1)}, u32[]{:S(2)}, u32[]{:S(2)}) %collective-permute-start.1) | collective-permute-done | bytes 2359328 | tf_op jit(solution)/shard_map/ppermute | solution.py:139
  532.5 4.4 fusion.171
  536.9 3.5 copy.200
  540.4 32.7 %reduce-scatter.3.cloned.1.call-done = f32[3,3,32,256]{3,2,1,0:T(8,128)} async-done(((f32[3,3,256,256]{3,2,1,0:T(8,128)}), f32[3,3,32,256]{3,2,1,0:T(8,128)}) %reduce-scatter.3.cloned.1.call-update) | async-done | bytes 294928 | tf_op jit(solution)/shard_map/reduce_scatter | solution.py:140
  (194 shorter events, 96.8 us)
Async XLA Ops:
  7.2 3.9 copy-start.4
  7.2 5.6 copy-start.45
  7.2 38.5 %all-gather.5.cloned.1.call-start = ((), (), s32[]{:S(2)}) async-start(), calls=%async_computation.2 | async-start | bytes 1966080 | tf_op jit(solution)/shard_map/all_gather | solution.py:28
  11.9 66.8 %all-gather.7.cloned.1.call-start = ((), (), s32[]{:S(2)}) async-start(), calls=%async_computation.3 | async-start | bytes 2654208 | tf_op jit(solution)/shard_map/all_gather | solution.py:144
  12.7 173.3 %all-gather.9.cloned.1.call-start = ((), (), s32[]{:S(2)}) async-start(), calls=%async_computation.4 | async-start | bytes 1966080 | tf_op jit(solution)/shard_map/all_gather | solution.py:28
  62.1 3.3 copy-start.10
  78.7 3.0 copy-start.27
  81.7 6.2 %copy-start.26 = (bf16[6,32,32,256]{3,2,1,0:T(8,128)(2,1)S(1)}, bf16[6,32,32,256]{3,2,1,0:T(8,128)(2,1)}, u32[]{:S(2)}) copy-start(bf16[6,32,32,256]{3,2,1,0:T(8,128)(2,1)} %get-tuple-element.27) | copy-start | bytes 9437188
  87.9 6.2 %copy-start.25 = (bf16[6,32,32,256]{3,2,1,0:T(8,128)(2,1)S(1)}, bf16[6,32,32,256]{3,2,1,0:T(8,128)(2,1)}, u32[]{:S(2)}) copy-start(bf16[6,32,32,256]{3,2,1,0:T(8,128)(2,1)} %get-tuple-element.25) | copy-start | bytes 9437188
  94.1 6.3 %copy-start.30 = (bf16[6,32,32,256]{3,2,1,0:T(8,128)(2,1)S(1)}, bf16[6,32,32,256]{3,2,1,0:T(8,128)(2,1)}, u32[]{:S(2)}) copy-start(bf16[6,32,32,256]{3,2,1,0:T(8,128)(2,1)} %get-tuple-element.39) | copy-start | bytes 9437188
  106.8 6.3 %copy-start.28 = (bf16[6,32,32,256]{3,2,1,0:T(8,128)(2,1)S(1)}, bf16[6,32,32,256]{3,2,1,0:T(8,128)(2,1)}, u32[]{:S(2)}) copy-start(bf16[6,32,32,256]{3,2,1,0:T(8,128)(2,1)} %get-tuple-element.38) | copy-start | bytes 9437188
  113.1 6.2 %copy-start.24 = (bf16[6,32,32,256]{3,2,1,0:T(8,128)(2,1)S(1)}, bf16[6,32,32,256]{3,2,1,0:T(8,128)(2,1)}, u32[]{:S(2)}) copy-start(bf16[6,32,32,256]{3,2,1,0:T(8,128)(2,1)} %get-tuple-element.65) | copy-start | bytes 9437188
  119.3 6.7 %copy-start.23 = (bf16[6,32,32,256]{3,2,1,0:T(8,128)(2,1)S(1)}, bf16[6,32,32,256]{3,2,1,0:T(8,128)(2,1)}, u32[]{:S(2)}) copy-start(bf16[6,32,32,256]{3,2,1,0:T(8,128)(2,1)} %get-tuple-element.64) | copy-start | bytes 9437188
  126.0 6.2 %copy-start.5 = (bf16[1,6,32,32,256]{4,3,2,1,0:T(8,128)(2,1)S(1)}, bf16[1,6,32,32,256]{4,3,2,1,0:T(8,128)(2,1)}, u32[]{:S(2)}) copy-start(bf16[1,6,32,32,256]{4,3,2,1,0:T(8,128)(2,1)} %param.4) | copy-start | bytes 9437188
  126.0 6.2 %copy-start.13 = (bf16[6,32,32,256]{3,2,1,0:T(8,128)(2,1)S(1)}, bf16[6,32,32,256]{3,2,1,0:T(8,128)(2,1)}, u32[]{:S(2)}) copy-start(bf16[6,32,32,256]{3,2,1,0:T(8,128)(2,1)} %get-tuple-element.66) | copy-start | bytes 9437188
  154.2 48.5 %copy-start.2 = (bf16[1,6,32,32,256]{4,2,1,3,0:T(8,128)(2,1)}, bf16[1,6,32,32,256]{4,2,1,3,0:T(8,128)(2,1)S(1)}, u32[]{:S(2)}) copy-start(bf16[1,6,32,32,256]{4,2,1,3,0:T(8,128)(2,1)S(1)} %get-tuple-element.60) | copy-start | bytes 9437188
  155.7 227.4 %all-gather.11.cloned.1.call-start = ((), (), s32[]{:S(2)}) async-start(), calls=%async_computation.5 | async-start | bytes 1966080 | tf_op jit(solution)/shard_map/all_gather | solution.py:33
  192.3 2.9 copy-start.35
  195.2 15.8 %copy-start = (bf16[1,6,33,34,256]{4,2,1,3,0:T(8,128)(2,1)}, bf16[1,6,33,34,256]{4,2,1,3,0:T(8,128)(2,1)S(1)}, u32[]{:S(2)}) copy-start(bf16[1,6,33,34,256]{4,2,1,3,0:T(8,128)(2,1)S(1)} %get-tuple-element.30) | copy-start | bytes 10340356
  203.3 18.5 %copy-start.34 = (bf16[6,32,32,256]{3,1,0,2:T(8,128)(2,1)}, bf16[6,32,32,256]{3,1,0,2:T(8,128)(2,1)S(1)}, u32[]{:S(2)}) copy-start(bf16[6,32,32,256]{3,1,0,2:T(8,128)(2,1)S(1)} %get-tuple-element.33) | copy-start | bytes 9437188
  203.3 22.0 %copy-start.32 = (bf16[6,32,32,256]{3,1,0,2:T(8,128)(2,1)}, bf16[6,32,32,256]{3,1,0,2:T(8,128)(2,1)S(1)}, u32[]{:S(2)}) copy-start(bf16[6,32,32,256]{3,1,0,2:T(8,128)(2,1)S(1)} %get-tuple-element.32) | copy-start | bytes 9437188
  250.6 3.8 copy-start.3
  258.5 4.3 copy-start.36
  329.6 3.8 copy-start.42
  339.7 200.7 %reduce-scatter.5.cloned.1.call-start = ((), (), s32[]{:S(2)}) async-start(), calls=%async_computation.7 | async-start | bytes 2654208 | tf_op jit(solution)/shard_map/reduce_scatter | solution.py:140
  339.8 2.8 copy-start.40
  341.1 4.9 copy-start.16
  342.6 3.5 copy-start.18
  342.6 6.5 %slice-start = ((s8[8355840]{0:T(1024)(128)(4,1)}), s8[4194304]{0:T(1024)(128)(4,1)S(1)}, s32[]{:S(2)}) async-start(s8[8355840]{0:T(1024)(128)(4,1)} %bitcast.433), calls=%async_computation.8 | async-start | bytes 8388608
  344.8 4.4 slice-start.1
  346.0 3.5 copy-start.15
  347.6 68.4 %collective-permute-start.2 = (f32[3,3,256,256]{3,2,1,0:T(8,128)}, f32[3,3,256,256]{3,2,1,0:T(8,128)S(1)}, u32[]{:S(2)}, u32[]{:S(2)}) collective-permute-start(f32[3,3,256,256]{3,2,1,0:T(8,128)} %pad_maximum_fusion.8), channel_id=1, source_target_pairs={{0,1},{1,0},{2,3},{3,2},{4,5},{5,4},{6,7},{7,6},{8,9},{9,8},{10,11... | collective-permute-start | bytes 7077896 | tf_op jit(solution)/shard_map/ppermute | solution.py:139
  351.7 2.6 copy-start.12
  391.4 3.0 copy-start.7
  391.4 5.1 slice-start.2
  396.5 2.6 copy-start.11
  411.0 2.6 copy-start.9
  413.6 2.4 copy-start.17
  413.6 2.4 copy-start.19
  417.5 53.0 %collective-permute-start.3 = (f32[3,3,256,256]{3,2,1,0:T(8,128)S(1)}, f32[3,3,256,256]{3,2,1,0:T(8,128)S(1)}, u32[]{:S(2)}, u32[]{:S(2)}) collective-permute-start(f32[3,3,256,256]{3,2,1,0:T(8,128)S(1)} %fusion.161), channel_id=1, source_target_pairs={{0,2},{1,3},{2,0},{3,1},{4,6},{5,7},{6,4},{7,5},{8,10},{9,11},{10,... | collective-permute-start | bytes 7077896 | tf_op jit(solution)/shard_map/ppermute | solution.py:139
  419.0 59.5 %copy-start.20 = (f32[1,3,256,256]{3,2,1,0:T(8,128)}, f32[1,3,256,256]{3,2,1,0:T(8,128)S(1)}, u32[]{:S(2)}) copy-start(f32[1,3,256,256]{3,2,1,0:T(8,128)S(1)} %maximum_bitcast_fusion.2) | copy-start | bytes 2359300
  419.1 59.4 %copy-start.21 = (f32[1,3,256,256]{3,2,1,0:T(8,128)}, f32[1,3,256,256]{3,2,1,0:T(8,128)S(1)}, u32[]{:S(2)}) copy-start(f32[1,3,256,256]{3,2,1,0:T(8,128)S(1)} %maximum_bitcast_fusion.1) | copy-start | bytes 2359300
  423.7 46.7 %copy-start.38 = (f32[3,3,256,256]{3,2,1,0:T(8,128)S(1)}, f32[3,3,256,256]{3,2,1,0:T(8,128)}, u32[]{:S(2)}) copy-start(f32[3,3,256,256]{3,2,1,0:T(8,128)} %copy-done.37) | copy-start | bytes 7077892
  423.8 54.7 %copy-start.22 = (f32[1,3,256,256]{3,2,1,0:T(8,128)}, f32[1,3,256,256]{3,2,1,0:T(8,128)S(1)}, u32[]{:S(2)}) copy-start(f32[1,3,256,256]{3,2,1,0:T(8,128)S(1)} %maximum_bitcast_fusion) | copy-start | bytes 2359300
  425.5 53.0 %collective-permute-start = (f32[3,3,256,256]{3,2,1,0:T(8,128)}, f32[3,3,256,256]{3,2,1,0:T(8,128)}, u32[]{:S(2)}, u32[]{:S(2)}) collective-permute-start(f32[3,3,256,256]{3,2,1,0:T(8,128)} %pad_maximum_fusion.7), channel_id=1, source_target_pairs={{0,1},{1,0},{2,3},{3,2},{4,5},{5,4},{6,7},{7,6},{8,9},{9,8},{10,11... | collective-permute-start | bytes 7077896 | tf_op jit(solution)/shard_map/ppermute | solution.py:139
  472.4 100.8 %reduce-scatter.3.cloned.1.call-start = ((), (), s32[]{:S(2)}) async-start(), calls=%async_computation.6 | async-start | bytes 2654208 | tf_op jit(solution)/shard_map/reduce_scatter | solution.py:140
  480.5 51.9 %collective-permute-start.1 = (f32[3,3,256,256]{3,2,1,0:T(8,128)S(1)}, f32[3,3,256,256]{3,2,1,0:T(8,128)S(1)}, u32[]{:S(2)}, u32[]{:S(2)}) collective-permute-start(f32[3,3,256,256]{3,2,1,0:T(8,128)S(1)} %fusion.162), channel_id=1, source_target_pairs={{0,2},{1,3},{2,0},{3,1},{4,6},{5,7},{6,4},{7,5},{8,10},{9,11},{10,... | collective-permute-start | bytes 7077896 | tf_op jit(solution)/shard_map/ppermute | solution.py:139
  532.5 4.4 copy-start.14
  (12 other events, 23.8 us)
Sparse Core Ops, SparseCore 0:
  12.0 33.5 all-gather.4
  47.2 31.4 all-gather.6
  155.8 30.0 all-gather.8
  339.9 43.2 all-gather.10
  472.5 37.0 reduce-scatter.4
  537.0 36.1 reduce-scatter.2
